TPU v7x, 32 devices: a whole 2x2x4 slice. The times are simulated.
32 devices in a mesh: member: 4 (over y, x), region: 8 (over z, core).
Axes of the slice: x: 2, y: 2, z: 4, core: 2. Of those that a mesh axis runs over, the one named last changes fastest.
Arguments:
- states: float32 [256, 49152], P('member', 'region'), may hold values from -6 to 6
- weights: float32 [256, 49152], P('member', 'region'), may hold values from -6 to 6
- obs_count: int32 [384], P('region'), may hold values from 0 to 32
- neighbours: int32 [384, 12], P('region'), may hold values from 0 to 383, as said below
Outputs:
- increments: float32 [256, 49152], P('member', 'region')
Inputs may be any that keep to these rules, and one draw needn't show every extreme that they name: `neighbours`: each row lists 12 distinct tiles, all within 8 tiles of its own tile counting cyclically over the 384 tiles; the list always holds the tile itself and the tiles exactly 8 before and after it, in a drawn order.
All inputs are finite; a program needn't handle non-finite values.
Results may differ from a plain program's by a relative error of at most 0.0003.
Values sent between devices are 32-bit elements; how exact they have to be, the bound alone decides.
A program may use at most 128 MiB of HBM per device.

v0:
```python
import jax
import jax.numpy as jnp
from jax import lax
from jax.sharding import PartitionSpec as P

TILE = 128
HALO_TILES = 8
TPD = 12


def extended_2(block, sides, width):
    for axis, dim in sides:
        count = lax.axis_size(axis)
        forward = [(i, i + 1) for i in range(count - 1)]
        forward.append((count - 1, 0))
        backward = [(target, source) for source, target in forward]
        low = lax.ppermute(
            lax.slice_in_dim(block, block.shape[dim] - width, None, axis=dim), axis, forward
        )
        high = lax.ppermute(lax.slice_in_dim(block, 0, width, axis=dim), axis, backward)
        block = jnp.concatenate([low, block, high], axis=dim)
    return block


def taper(offset, tile):
    rows = jnp.arange(tile, dtype=jnp.float32)
    spread = tile * offset[:, None, None] + rows[None, None, :] - rows[None, :, None]
    scaled = spread / (2.0 * tile)
    return 1.0 / (1.0 + scaled * scaled)


def shards(states, weights, obs_count, neighbours):
    member_count = lax.axis_size("member")
    region_count = lax.axis_size("region")
    member_part, local_rows = states.shape
    local_tiles = local_rows // TILE
    counts = obs_count.astype(jnp.float32)
    factor = counts / (counts + 8.0)
    scaled = (weights.reshape(member_part, local_tiles, TILE) * factor[None, :, None]).reshape(
        member_part, local_rows
    )
    stacked = jnp.stack([states, scaled])
    rim = HALO_TILES * TILE
    block = TPD * TILE
    padded = extended_2(stacked, (("region", 2),), rim)
    own_block = lax.all_to_all(stacked, "member", split_axis=2, concat_axis=1, tiled=True)
    extended = extended_2(own_block, (("member", 2),), rim)
    below, above = (
        lax.all_gather(padded[:, :, :rim], "member", axis=1, tiled=True),
        lax.all_gather(padded[:, :, rim + local_rows :], "member", axis=1, tiled=True),
    )
    position = lax.axis_index("member")
    lower = jnp.where(position == 0, below, extended[:, :, :rim])
    upper = jnp.where(position == member_count - 1, above, extended[:, :, rim + block :])
    window = jnp.concatenate([lower, extended[:, :, rim : rim + block], upper], axis=2)
    members = window.shape[1]
    anomaly = window[0] - jnp.mean(window[0], axis=0, keepdims=True)
    window_weights = window[1]
    tiles_all = TPD * member_count * region_count
    first_tile = (lax.axis_index("region") * member_count + lax.axis_index("member")) * TPD
    lists = lax.dynamic_slice_in_dim(neighbours, lax.axis_index("member") * TPD, TPD, 0)
    local_ids = (lists - first_tile + HALO_TILES) % tiles_all
    span_count = 2 * HALO_TILES + 1
    tile_places = jnp.arange(TPD, dtype=jnp.int32)
    shift_places = jnp.arange(span_count, dtype=jnp.int32)
    wanted = tile_places[:, None, None] + shift_places[None, None, :]
    keep_table = jnp.sum((local_ids[:, :, None] == wanted).astype(jnp.float32), axis=1)
    mine = anomaly[:, rim : rim + block].reshape(members, TPD, TILE)

    def add_offset(shift, total):
        others = lax.dynamic_slice_in_dim(anomaly, shift * TILE, block, 1).reshape(
            members, TPD, TILE
        )
        other_weights = lax.dynamic_slice_in_dim(window_weights, shift * TILE, block, 1).reshape(
            members, TPD, TILE
        )
        covar = jnp.einsum("mti,mtj->tij", mine, others, precision=lax.Precision.HIGHEST) / (
            members - 1.0
        )
        offset = jnp.full((TPD,), shift - HALO_TILES).astype(jnp.float32)
        keep = lax.dynamic_index_in_dim(keep_table, shift, 1, keepdims=False)
        coefficient = taper(offset, TILE) * covar * keep[:, None, None]
        return total + jnp.einsum(
            "mtj,tij->mti", other_weights, coefficient, precision=lax.Precision.HIGHEST
        )

    total = lax.fori_loop(0, span_count, add_offset, jnp.zeros((members, TPD, TILE), jnp.float32))
    returned = lax.all_to_all(
        total.reshape(members, block), "member", split_axis=0, concat_axis=1, tiled=True
    )
    return returned


def solution(mesh):
    placed = (P("member", "region"), P("member", "region"), P("region"), P("region", None))
    return jax.shard_map(
        shards, mesh=mesh, in_specs=placed, out_specs=P("member", "region"), check_vma=False
    )
```

profile of v0, /device:TPU:0, one launch (start us, length us, event | category | flops | bytes accessed | tf_op | source)
XLA Modules:
  0.0 480.4 jit_solution(8024815179831741481)
XLA Ops:
  10.3 11.0 %collective-permute-done = f32[2,64,1024]{2,1,0:T(8,128)} collective-permute-done((f32[2,64,1024]{2,1,0:T(8,128)S(1)}, f32[2,64,1024]{2,1,0:T(8,128)}, u32[]{:S(2)}, u32[]{:S(2)}) %collective-permute-start) | collective-permute-done | bytes 524320 | tf_op jit(solution)/shard_map/ppermute | solution.py:17
  23.2 8.5 %copy.49 = f32[2,64,6144]{1,0,2:T(2,128)} copy(f32[2,64,6144]{2,1,0:T(8,128)} %pad_maximum_fusion.1) | data formatting | bytes 6291456 | tf_op jit(solution)/shard_map/stack | solution.py:42
  31.8 9.0 %reshape.73 = f32[4,1,196608]{2,1,0:T(1,128)} reshape(f32[6144,2,64]{2,1,0:T(2,128)} %bitcast.56) | data formatting | bytes 6291456
  45.0 7.0 %collective-permute-done.2 = f32[2,64,1024]{2,1,0:T(8,128)} collective-permute-done((f32[2,64,1024]{2,1,0:T(8,128)}, f32[2,64,1024]{2,1,0:T(8,128)}, u32[]{:S(2)}, u32[]{:S(2)}) %collective-permute-start.2) | collective-permute-done | bytes 524320 | tf_op jit(solution)/shard_map/ppermute | solution.py:20
  52.1 38.0 %all-to-all-done = f32[4,1,196608]{2,1,0:T(1,128)S(1)} async-done(((f32[4,1,196608]{2,1,0:T(1,128)}), f32[4,1,196608]{2,1,0:T(1,128)S(1)}, u32[]{:S(2)}, u32[]{:S(2)}) %all-to-all-start) | async-done | bytes 3145760 | tf_op jit(solution)/shard_map/all_to_all | solution.py:46
  90.5 10.7 %reduce.1 = f32[4,196608]{1,0:T(4,128)} reduce(f32[4,1,196608]{2,1,0:T(1,128)S(1)} %all-to-all-done, f32[]{:T(128)} %broadcast.103), dimensions={1}, to_apply=%all_to_all.27.reduce_sub_computation | reduce | bytes 6291460 | tf_op jit(solution)/shard_map/all_to_all | solution.py:46
  101.2 9.5 %reshape.74 = f32[6144,2,64]{2,1,0:T(2,128)} reshape(f32[4,196608]{1,0:T(4,128)} %reduce.1) | data formatting | bytes 6291456
  110.6 9.6 %copy.62 = f32[2,64,4,1536]{3,2,1,0:T(4,128)} copy(f32[2,64,4,1536]{1,0,3,2:T(2,128)} %bitcast.57) | data formatting | bytes 6291456 | tf_op jit(solution)/shard_map/all_to_all | solution.py:46
  128.8 46.4 %collective-permute-done.1 = f32[2,256,1024]{2,1,0:T(8,128)} collective-permute-done((f32[2,256,1024]{2,1,0:T(8,128)}, f32[2,256,1024]{2,1,0:T(8,128)}, u32[]{:S(2)}, u32[]{:S(2)}) %collective-permute-start.1) | collective-permute-done | bytes 2097184 | tf_op jit(solution)/shard_map/ppermute | solution.py:17
  178.7 39.3 %collective-permute-done.3 = f32[2,256,1024]{2,1,0:T(8,128)} collective-permute-done((f32[2,256,1024]{2,1,0:T(8,128)}, f32[2,256,1024]{2,1,0:T(8,128)}, u32[]{:S(2)}, u32[]{:S(2)}) %collective-permute-start.3) | collective-permute-done | bytes 2097184 | tf_op jit(solution)/shard_map/ppermute | solution.py:20
  227.4 219.7 %while.16 = (s32[]{:T(128)}, f32[256,12,128]{0,2,1:T(8,128)}, f32[256,3584]{1,0:T(8,128)}, f32[256,12,128]{2,0,1:T(8,128)}, f32[12,17]{0,1:T(8,128)S(1)}, /*inde...) while((s32[]{:T(128)}, f32[256,12,128]{0,2,1:T(8,128)}, ...), condition=%wide.region_3.4_spmd.clone, body=%wide.region_2.3_spmd.clone.sunk | while | flops 1210318976 | bytes 22021480 | solution.py:87
  231.2 4.4 fusion.22
  243.6 4.4 fusion.22
  256.5 4.4 fusion.22
  269.5 4.4 fusion.22
  282.4 4.4 fusion.22
  295.4 4.4 fusion.22
  308.3 4.4 fusion.22
  321.3 4.4 fusion.22
  334.2 4.4 fusion.22
  347.2 4.4 fusion.22
  360.1 4.4 fusion.22
  437.9 4.4 fusion.22
  450.6 21.7 %all_to_all.37 = f32[4,64,1536]{2,1,0:T(8,128)S(1)} all-to-all(f32[4,64,1536]{2,1,0:T(8,128)} %all_to_all.31), channel_id=1, replica_groups=mesh['member'=4,'region'=8] {'member'}, dimensions={0} | all-to-all | bytes 3145728 | tf_op jit(solution)/shard_map/all_to_all | solution.py:88
  (152 shorter events, 202.8 us)
Async XLA Ops:
  6.5 2.4 copy-start.2
  6.5 122.2 %all-gather.3.cloned.1.call-start = ((), (), s32[]{:S(2)}) async-start(), calls=%async_computation.2 | async-start | bytes 2621440 | tf_op jit(solution)/shard_map/all_gather | solution.py:49
  9.8 11.5 %collective-permute-start = (f32[2,64,1024]{2,1,0:T(8,128)S(1)}, f32[2,64,1024]{2,1,0:T(8,128)}, u32[]{:S(2)}, u32[]{:S(2)}) collective-permute-start(f32[2,64,1024]{2,1,0:T(8,128)S(1)} %get-tuple-element.229), channel_id=1, source_target_pairs={{0,1},{1,2},{2,3},{3,4},{4,5},{5,6},{6,7},{7,0},{8,9},{9,10},{10,1... | collective-permute-start | bytes 1572872 | tf_op jit(solution)/shard_map/ppermute | solution.py:17
  40.8 49.2 %all-to-all-start = ((f32[4,1,196608]{2,1,0:T(1,128)}), f32[4,1,196608]{2,1,0:T(1,128)S(1)}, u32[]{:S(2)}, u32[]{:S(2)}) async-start(f32[4,1,196608]{2,1,0:T(1,128)} %reshape.73), calls=%async_computation | async-start | bytes 6291456 | tf_op jit(solution)/shard_map/all_to_all | solution.py:46
  45.0 133.7 %all-gather.5.cloned.1.call-start = ((), (), s32[]{:S(2)}) async-start(), calls=%async_computation.3 | async-start | bytes 2621440 | tf_op jit(solution)/shard_map/all_gather | solution.py:50
  45.0 7.0 %collective-permute-start.2 = (f32[2,64,1024]{2,1,0:T(8,128)}, f32[2,64,1024]{2,1,0:T(8,128)}, u32[]{:S(2)}, u32[]{:S(2)}) collective-permute-start(f32[2,64,1024]{2,1,0:T(8,128)} %get-tuple-element.230), channel_id=1, source_target_pairs={{1,0},{2,1},{3,2},{4,3},{5,4},{6,5},{7,6},{0,7},{9,8},{10,9},{11,1... | collective-permute-start | bytes 1572872 | tf_op jit(solution)/shard_map/ppermute | solution.py:20
  123.0 5.4 %copy-start.3 = (s32[48,12]{0,1:T(8,128)S(1)}, s32[48,12]{0,1:T(8,128)}, u32[]{:S(2)}) copy-start(s32[48,12]{0,1:T(8,128)} %param.9) | copy-start | bytes 6916
  125.5 49.7 %collective-permute-start.1 = (f32[2,256,1024]{2,1,0:T(8,128)}, f32[2,256,1024]{2,1,0:T(8,128)}, u32[]{:S(2)}, u32[]{:S(2)}) collective-permute-start(f32[2,256,1024]{2,1,0:T(8,128)} %get-tuple-element.227), channel_id=1, source_target_pairs={{0,8},{8,16},{16,24},{24,0},{1,9},{9,17},{17,25},{25,1},{2,10},{10... | collective-permute-start | bytes 6291464 | tf_op jit(solution)/shard_map/ppermute | solution.py:17
  126.9 91.1 %collective-permute-start.3 = (f32[2,256,1024]{2,1,0:T(8,128)}, f32[2,256,1024]{2,1,0:T(8,128)}, u32[]{:S(2)}, u32[]{:S(2)}) collective-permute-start(f32[2,256,1024]{2,1,0:T(8,128)} %get-tuple-element.228), channel_id=1, source_target_pairs={{8,0},{16,8},{24,16},{0,24},{9,1},{17,9},{25,17},{1,25},{10,2},{18... | collective-permute-start | bytes 6291464 | tf_op jit(solution)/shard_map/ppermute | solution.py:20
  178.7 41.4 %copy-start.1 = (f32[2,256,1024]{2,1,0:T(8,128)S(1)}, f32[2,256,1024]{2,1,0:T(8,128)}, u32[]{:S(2)}) copy-start(f32[2,256,1024]{2,1,0:T(8,128)} %broadcast_select_fusion.1) | copy-start | bytes 6291460
  223.3 1.8 copy-start
Sparse Core Ops, SparseCore 0:
  21.4 62.4 all-gather.2
  85.8 34.5 all-gather.4
where the time goes:
time: 482 us; the launch traced here: 480 us
  matrix products  148 us (31%)
  waiting for transfers between devices  142 us (29%)
  local copies, waits for them, and re-layouts  123 us (26%)
  other arithmetic  24.8 us (5%)
  blocking collectives  21.7 us (5%)
  between operations  13.5 us (3%)
  starting transfers between devices  7.63 us (2%)
    dot_general x17, matrix products, add_offset(): jnp.einsum('mti,mtj->tij', mine, others, precision=lax.Precision.HIGHEST)  75.3 us
    dot_general x17, matrix products, add_offset(): jnp.einsum('mtj,tij->mti', other_weights, coefficient, precision=lax.Prec...  72.7 us
    ppermute x2, waiting for transfers between devices, extended_2(): lax.ppermute(lax.slice_in_dim(block, block.shape[dim] - width, None, axis...  57.4 us
    ppermute x2, waiting for transfers between devices, extended_2(): lax.ppermute(lax.slice_in_dim(block, 0, width, axis=dim), axis, backward)  46.3 us
    dynamic_slice x34, local copies, waits for them, and re-layouts, add_offset(): lax.dynamic_slice_in_dim(window_weights, shift * TILE, block, 1)  43.3 us
    all_to_all x1, waiting for transfers between devices, shards(): lax.all_to_all(stacked, 'member', split_axis=2, concat_axis=1, tiled=True)  38 us
    dynamic_slice x17, local copies, waits for them, and re-layouts, add_offset(): lax.dynamic_slice_in_dim(anomaly, shift * TILE, block, 1)  27.8 us
    unnamed x12, local copies, waits for them, and re-layouts  22.2 us
  transfers between devices with their start and end apart: 7, of which 5 were waited for; matrix products, arithmetic and copies ran while one was open for 12% of the time, Pallas kernels for 0%

commit v1 on v0

--- a/solution.py
+++ b/solution.py
@@ -1,6 +1,8 @@
 import jax
 import jax.numpy as jnp
 from jax import lax
+from jax.experimental import pallas as pl
+from jax.experimental.pallas import tpu as pltpu
 from jax.sharding import PartitionSpec as P
 
 TILE = 128
@@ -91,8 +93,161 @@
     return returned
 
 
+BLOCK = 2 * TILE
+SPAN = HALO_TILES + 1
+RIM = HALO_TILES * TILE
+
+
+def split(value):
+    high = value.astype(jnp.bfloat16)
+    return high, (value - high.astype(jnp.float32)).astype(jnp.bfloat16)
+
+
+def dot(left, right):
+    return jnp.dot(left, right, preferred_element_type=jnp.float32)
+
+
+def fill_taper(taper_ref, members):
+    rows = lax.broadcasted_iota(jnp.int32, (BLOCK, BLOCK), 0)
+    columns = lax.broadcasted_iota(jnp.int32, (BLOCK, BLOCK), 1)
+    for k in range(SPAN):
+        spread = (columns - rows + (2 * k - HALO_TILES) * TILE).astype(jnp.float32) / (2.0 * TILE)
+        taper_ref[k] = 1.0 / ((1.0 + spread * spread) * (members - 1.0))
+
+
+def prepare_states(value, block, own, low_ref, high_ref, low_t_ref, high_t_ref):
+    anomaly = value - jnp.mean(value, axis=0, keepdims=True)
+    high_ref[block], low_ref[block] = split(anomaly)
+    if own is not None:
+        high_t_ref[own], low_t_ref[own] = split(anomaly.T)
+
+
+def prepare_weights(value, block, weight_ref):
+    high = value.astype(jnp.bfloat16).astype(jnp.float32)
+    weight_ref[block] = jnp.concatenate([high, value - high], axis=0).T.astype(jnp.bfloat16)
+
+
+def pair_increment(pair, keep_ref, low_ref, high_ref, low_t_ref, high_t_ref, weight_ref, taper_ref):
+    total = None
+    for k in range(SPAN):
+        left_high, left_low = high_t_ref[pair], low_t_ref[pair]
+        right_high, right_low = high_ref[pair + k], low_ref[pair + k]
+        covar = dot(left_high, right_high) + dot(left_low, right_high) + dot(left_high, right_low)
+        scaled = covar * taper_ref[k]
+        rows = []
+        for s in range(2):
+            rows.append(
+                jnp.concatenate(
+                    [
+                        scaled[s * TILE : (s + 1) * TILE, t * TILE : (t + 1) * TILE]
+                        * keep_ref[2 * pair + s, 2 * k + t + 1 - s]
+                        for t in range(2)
+                    ],
+                    axis=1,
+                )
+            )
+        high, low = split(jnp.concatenate(rows, axis=0))
+        weight = weight_ref[pair + k]
+        term = dot(high, weight) + dot(low, weight)
+        total = term if total is None else total + term
+    half = total.shape[1] // 2
+    return (total[:, :half] + total[:, half:]).T
+
+
+def local_kernel(states_ref, weights_ref, keep_ref, out_ref, low_ref, high_ref, low_t_ref, high_t_ref, weight_ref, taper_ref):
+    members, window = states_ref.shape
+    blocks = window // BLOCK
+    rim = RIM // BLOCK
+    pairs = blocks - 2 * rim
+    fill_taper(taper_ref, members)
+
+    def prepare(block, own):
+        columns = pl.ds(pl.multiple_of(block * BLOCK, BLOCK), BLOCK)
+        prepare_states(states_ref[:, columns], block, own, low_ref, high_ref, low_t_ref, high_t_ref)
+        prepare_weights(weights_ref[:, columns], block, weight_ref)
+
+    pl.loop(0, rim)(lambda b: prepare(b, None))
+    pl.loop(0, pairs)(lambda b: prepare(b + rim, b))
+    pl.loop(0, rim)(lambda b: prepare(b + rim + pairs, None))
+
+    @pl.loop(0, pairs)
+    def _(pair):
+        columns = pl.ds(pl.multiple_of(pair * BLOCK, BLOCK), BLOCK)
+        out_ref[:, columns] = pair_increment(
+            pair, keep_ref, low_ref, high_ref, low_t_ref, high_t_ref, weight_ref, taper_ref
+        )
+
+
+def scratch_of(members, part, pairs):
+    rim = RIM // BLOCK
+    blocks = pairs + 2 * rim
+    bf16 = jnp.bfloat16
+    return [
+        pltpu.VMEM((blocks, members, BLOCK), bf16),
+        pltpu.VMEM((blocks, members, BLOCK), bf16),
+        pltpu.VMEM((pairs, BLOCK, members), bf16),
+        pltpu.VMEM((pairs, BLOCK, members), bf16),
+        pltpu.VMEM((blocks, BLOCK, 2 * part), bf16),
+        pltpu.VMEM((SPAN, BLOCK, BLOCK), jnp.float32),
+    ]
+
+
+def keep_table_of(neighbours, factor_window, tiles_all):
+    local_tiles = neighbours.shape[0]
+    first = lax.axis_index("region") * local_tiles
+    own = first + jnp.arange(local_tiles, dtype=jnp.int32)
+    shift = (neighbours - own[:, None] + HALO_TILES + 1) % tiles_all
+    places = jnp.arange(2 * SPAN + 2, dtype=jnp.int32)
+    return jnp.sum((shift[:, :, None] == places).astype(jnp.float32), axis=1)
+
+
+def local_increment(states, weights, keep):
+    members, window = states.shape
+    part = weights.shape[0]
+    pairs = window // BLOCK - 2 * (RIM // BLOCK)
+    vmem = pl.BlockSpec(memory_space=pltpu.VMEM)
+    return pl.pallas_call(
+        local_kernel,
+        out_shape=jax.ShapeDtypeStruct((part, pairs * BLOCK), jnp.float32),
+        in_specs=[vmem, vmem, pl.BlockSpec(memory_space=pltpu.SMEM)],
+        out_specs=vmem,
+        scratch_shapes=scratch_of(members, part, pairs),
+        compiler_params=pltpu.CompilerParams(vmem_limit_bytes=60 * 1024 * 1024),
+    )(states, weights, keep)
+
+
+def region_shards(states, weights, obs_count, neighbours):
+    region_count = lax.axis_size("region")
+    part, local_rows = states.shape
+    counts = obs_count.astype(jnp.float32)
+    factor = counts / (counts + 8.0)
+    scaled = (weights.reshape(part, local_rows // TILE, TILE) * factor[None, :, None]).reshape(part, local_rows)
+    gathered = lax.all_gather(states, "member", axis=0, tiled=True)
+    window = extended_2(gathered, (("region", 1),), RIM)
+    weight_window = extended_2(scaled, (("region", 1),), RIM)
+    keep = keep_table_of(neighbours, None, region_count * (local_rows // TILE))
+    return local_increment(window, weight_window, keep)
+
+
+def fits(states, weights, obs_count, neighbours):
+    part, local_rows = states.shape
+    members = part * lax.axis_size("member")
+    window = local_rows + 2 * RIM
+    return (
+        local_rows % RIM == 0
+        and local_rows >= RIM
+        and members % 128 == 0
+        and part % 64 == 0
+        and window * (members * 12 + part * 16) <= 46 * 1024 * 1024
+    )
+
+
+def either(*arguments):
+    return region_shards(*arguments) if fits(*arguments) else shards(*arguments)
+
+
 def solution(mesh):
     placed = (P("member", "region"), P("member", "region"), P("region"), P("region", None))
     return jax.shard_map(
-        shards, mesh=mesh, in_specs=placed, out_specs=P("member", "region"), check_vma=False
-    )
+        either, mesh=mesh, in_specs=placed, out_specs=P("member", "region"), check_vma=False
+    )

time: 482 us -> 224 us (0.46)
  matrix products: 148 us -> 0 us
  local copies, waits for them, and re-layouts: 123 us -> 4.64 us
  Pallas kernels: 0 us -> 99.7 us
  waiting for transfers between devices: 142 us -> 89.2 us
  blocking collectives: 21.7 us -> 0 us
  other arithmetic: 24.8 us -> 7.95 us
    dot_general x34 -> x0, matrix products: 148 us -> none  [the longest x17 75.3 us: add_offset(): jnp.einsum('mti,mtj->tij', mine, others, precision=lax.Precision.HIGHEST)]
    pallas_call x0 -> x1, Pallas kernels: none -> 99.7 us  [local_increment(): pl.pallas_call(local_kernel, out_shape=jax.ShapeDtypeStruct((part, pairs...]
    dynamic_slice x51 -> x0, local copies, waits for them, and re-layouts: 71.2 us -> none  [the longest x34 43.3 us: add_offset(): lax.dynamic_slice_in_dim(window_weights, shift * TILE, block, 1)]
    all_gather x2 -> x1, waiting for transfers between devices: 0.01 us -> 68.5 us  [region_shards(): gathered = lax.all_gather(states, 'member', axis=0, tiled=True)]
    ppermute x2, waiting for transfers between devices: 46.3 us -> 0.01 us  [extended_2(): lax.ppermute(lax.slice_in_dim(block, 0, width, axis=dim), axis, backward)]
    all_to_all x1 -> x0, waiting for transfers between devices: 38 us -> none  [shards(): lax.all_to_all(stacked, 'member', split_axis=2, concat_axis=1, tiled=True)]
    ppermute x2, waiting for transfers between devices: 57.4 us -> 19.9 us  [extended_2(): lax.ppermute(lax.slice_in_dim(block, block.shape[dim] - width, None, axis...]
    unnamed x12 -> x4, local copies, waits for them, and re-layouts: 22.2 us -> 0.01 us
  transfers between devices with their start and end apart: 7 -> 5, of which waited for: 5 -> 2; matrix products, arithmetic and copies ran while one was open for 12% -> 3% of each run, Pallas kernels for 0% -> 0%
where the time goes in v1:
time: 224 us; the launch traced here: 223 us
  Pallas kernels  99.7 us (45%)
  waiting for transfers between devices  89.2 us (40%)
  between operations  13.4 us (6%)
  starting transfers between devices  8.07 us (4%)
  other arithmetic  7.95 us (4%)
  local copies, waits for them, and re-layouts  4.64 us (2%)
    pallas_call x1, Pallas kernels, local_increment(): pl.pallas_call(local_kernel, out_shape=jax.ShapeDtypeStruct((part, pairs...  99.7 us
    all_gather x1, waiting for transfers between devices, region_shards(): gathered = lax.all_gather(states, 'member', axis=0, tiled=True)  68.5 us
    ppermute x2, waiting for transfers between devices, extended_2(): lax.ppermute(lax.slice_in_dim(block, block.shape[dim] - width, None, axis...  19.9 us
    ppermute x2, starting transfers between devices, extended_2(): lax.ppermute(lax.slice_in_dim(block, 0, width, axis=dim), axis, backward)  7.57 us
    concatenate x2, other arithmetic, extended_2(): block = jnp.concatenate([low, block, high], axis=dim)  7.13 us
  transfers between devices with their start and end apart: 5, of which 2 were waited for; matrix products, arithmetic and copies ran while one was open for 3% of the time, Pallas kernels for 0%

profile of v1, /device:TPU:0, one launch (start us, length us, event | category | flops | bytes accessed | tf_op | source)
XLA Modules:
  0.0 222.9 jit_solution(6032293341674736641)
XLA Ops:
  6.5 0.0 copy-start
  6.5 0.0 all-gather.2.cloned.1.call-start
  6.5 0.7 all-gather.2.cloned.1.call-update
  7.3 0.7 add_divide_fusion
  7.9 0.1 broadcast_bitcast_fusion
  8.0 0.0 copy-done
  8.0 0.0 copy-start.1
  8.0 0.1 broadcast_multiply_fusion
  8.1 0.8 fusion.1
  8.9 0.5 collective-permute-start.2
  9.4 4.0 %collective-permute-start.3 = (f32[64,1024]{1,0:T(8,128)S(1)}, f32[64,1024]{1,0:T(8,128)S(1)}, u32[]{:S(2)}, u32[]{:S(2)}) collective-permute-start(f32[64,1024]{1,0:T(8,128)S(1)} %get-tuple-element.8), channel_id=1, source_target_pairs={{1,0},{2,1},{3,2},{4,3},{5,4},{6,5},{7,6},{0,7},{9,8},{10,9},{11,1... | collective-permute-start | bytes 786440 | tf_op jit(solution)/shard_map/ppermute | solution.py:22
  13.4 0.0 copy-done.1
  13.4 68.5 %all-gather.2.cloned.1.call-done = f32[256,6144]{1,0:T(8,128)} async-done(((f32[64,6144]{1,0:T(8,128)}), f32[256,6144]{1,0:T(8,128)}) %all-gather.2.cloned.1.call-update) | async-done | bytes 6291472 | tf_op jit(solution)/shard_map/all_gather | solution.py:225
  82.0 3.1 %fusion = (f32[256,1024]{1,0:T(8,128)}, f32[256,1024]{1,0:T(8,128)}) fusion(f32[256,6144]{1,0:T(8,128)} %all-gather.2.cloned.1.call-done), kind=kLoop, calls=%fused_computation.10 | loop fusion | bytes 4194304 | tf_op jit(solution)/shard_map/slice | solution.py:20
  85.1 0.0 collective-permute-start
  85.1 3.5 %collective-permute-start.1 = (f32[256,1024]{1,0:T(8,128)}, f32[256,1024]{1,0:T(8,128)}, u32[]{:S(2)}, u32[]{:S(2)}) collective-permute-start(f32[256,1024]{1,0:T(8,128)} %get-tuple-element.6), channel_id=1, source_target_pairs={{1,0},{2,1},{3,2},{4,3},{5,4},{6,5},{7,6},{0,7},{9,8},{10,9},{11,1... | collective-permute-start | bytes 3145736 | tf_op jit(solution)/shard_map/ppermute | solution.py:22
  88.6 0.7 copy.6.keep_ref
  89.3 0.0 collective-permute-done.2
  89.3 0.0 collective-permute-done.3
  89.3 1.5 pad_maximum_fusion.1.weights_ref
  90.8 19.9 %collective-permute-done = f32[256,1024]{1,0:T(8,128)S(1)} collective-permute-done((f32[256,1024]{1,0:T(8,128)}, f32[256,1024]{1,0:T(8,128)S(1)}, u32[]{:S(2)}, u32[]{:S(2)}) %collective-permute-start) | collective-permute-done | bytes 1048608 | tf_op jit(solution)/shard_map/ppermute | solution.py:19
  110.7 0.0 collective-permute-done.1
  110.7 5.7 %pad_maximum_fusion.states_ref = f32[256,8192]{1,0:T(8,128)} fusion(f32[256,1024]{1,0:T(8,128)} %collective-permute-done.1, f32[256,6144]{1,0:T(8,128)} %all-gather.2.cloned.1.call-done, f32[256,1024]{1,0:T(8,128)S(1)} %collective-permute-done), kind=kLoop, calls=%fused_computation | loop fusion | flops 4194304 | bytes 16777216 | tf_op jit(solution)/shard_map/concatenate | solution.py:23
  116.4 99.7 %shard_map.46 = f32[64,6144]{1,0:T(8,128)} custom-call(f32[256,8192]{1,0:T(8,128)} %pad_maximum_fusion.states_ref, f32[64,8192]{1,0:T(8,128)} %pad_maximum_fusion.1.weights_ref, f32[48,20]{1,0:T(8,128)} %copy.6.keep_ref), custom_call_target="tpu_custom_call" | custom-call | tf_op jit(solution)/shard_map/pallas_call | solution.py:209
  (3 shorter events, 0.0 us)
Async XLA Ops:
  6.5 1.5 copy-start
  6.5 75.4 %all-gather.2.cloned.1.call-start = ((), (), s32[]{:S(2)}) async-start(), calls=%async_computation | async-start | bytes 7864320 | tf_op jit(solution)/shard_map/all_gather | solution.py:225
  8.0 5.4 %copy-start.1 = (s32[48,12]{0,1:T(8,128)S(1)}, s32[48,12]{0,1:T(8,128)}, u32[]{:S(2)}) copy-start(s32[48,12]{0,1:T(8,128)} %param.7) | copy-start | bytes 6916
  8.9 80.4 %collective-permute-start.2 = (f32[64,1024]{1,0:T(8,128)}, f32[64,1024]{1,0:T(8,128)S(1)}, u32[]{:S(2)}, u32[]{:S(2)}) collective-permute-start(f32[64,1024]{1,0:T(8,128)} %get-tuple-element.7), channel_id=1, source_target_pairs={{0,1},{1,2},{2,3},{3,4},{4,5},{5,6},{6,7},{7,0},{8,9},{9,10},{10,1... | collective-permute-start | bytes 786440 | tf_op jit(solution)/shard_map/ppermute | solution.py:19
  9.4 80.0 %collective-permute-start.3 = (f32[64,1024]{1,0:T(8,128)S(1)}, f32[64,1024]{1,0:T(8,128)S(1)}, u32[]{:S(2)}, u32[]{:S(2)}) collective-permute-start(f32[64,1024]{1,0:T(8,128)S(1)} %get-tuple-element.8), channel_id=1, source_target_pairs={{1,0},{2,1},{3,2},{4,3},{5,4},{6,5},{7,6},{0,7},{9,8},{10,9},{11,1... | collective-permute-start | bytes 786440 | tf_op jit(solution)/shard_map/ppermute | solution.py:22
  85.1 25.6 %collective-permute-start = (f32[256,1024]{1,0:T(8,128)}, f32[256,1024]{1,0:T(8,128)S(1)}, u32[]{:S(2)}, u32[]{:S(2)}) collective-permute-start(f32[256,1024]{1,0:T(8,128)} %get-tuple-element.5), channel_id=1, source_target_pairs={{0,1},{1,2},{2,3},{3,4},{4,5},{5,6},{6,7},{7,0},{8,9},{9,10},{10,1... | collective-permute-start | bytes 3145736 | tf_op jit(solution)/shard_map/ppermute | solution.py:19
  85.1 25.6 %collective-permute-start.1 = (f32[256,1024]{1,0:T(8,128)}, f32[256,1024]{1,0:T(8,128)}, u32[]{:S(2)}, u32[]{:S(2)}) collective-permute-start(f32[256,1024]{1,0:T(8,128)} %get-tuple-element.6), channel_id=1, source_target_pairs={{1,0},{2,1},{3,2},{4,3},{5,4},{6,5},{7,6},{0,7},{9,8},{10,9},{11,1... | collective-permute-start | bytes 3145736 | tf_op jit(solution)/shard_map/ppermute | solution.py:22
Sparse Core Ops, SparseCore 0:
  9.2 72.7 all-gather.1

commit v2 on v1

--- a/solution.py
+++ b/solution.py
@@ -127,55 +127,25 @@
     weight_ref[block] = jnp.concatenate([high, value - high], axis=0).T.astype(jnp.bfloat16)
 
 
-def pair_increment(pair, keep_ref, low_ref, high_ref, low_t_ref, high_t_ref, weight_ref, taper_ref):
-    total = None
+def pair_rows(pair, keep_ref, low_ref, high_ref, low_t_ref, high_t_ref, taper_ref, x_high_ref, x_low_ref):
     for k in range(SPAN):
         left_high, left_low = high_t_ref[pair], low_t_ref[pair]
         right_high, right_low = high_ref[pair + k], low_ref[pair + k]
         covar = dot(left_high, right_high) + dot(left_low, right_high) + dot(left_high, right_low)
         scaled = covar * taper_ref[k]
-        rows = []
         for s in range(2):
-            rows.append(
-                jnp.concatenate(
-                    [
-                        scaled[s * TILE : (s + 1) * TILE, t * TILE : (t + 1) * TILE]
-                        * keep_ref[2 * pair + s, 2 * k + t + 1 - s]
-                        for t in range(2)
-                    ],
-                    axis=1,
-                )
-            )
-        high, low = split(jnp.concatenate(rows, axis=0))
-        weight = weight_ref[pair + k]
-        term = dot(high, weight) + dot(low, weight)
-        total = term if total is None else total + term
+            for t in range(2):
+                rows, columns = slice(s * TILE, (s + 1) * TILE), slice(t * TILE, (t + 1) * TILE)
+                value = scaled[rows, columns] * keep_ref[2 * pair + s, 2 * k + t + 1 - s]
+                place = slice((2 * k + t) * TILE, (2 * k + t + 1) * TILE)
+                x_high_ref[rows, place], x_low_ref[rows, place] = split(value)
+
+
+def pair_apply(pair, weight_ref, x_high_ref, x_low_ref):
+    weight = weight_ref[pl.ds(pair, SPAN)].reshape(SPAN * BLOCK, weight_ref.shape[2])
+    total = dot(x_high_ref[...], weight) + dot(x_low_ref[...], weight)
     half = total.shape[1] // 2
     return (total[:, :half] + total[:, half:]).T
-
-
-def local_kernel(states_ref, weights_ref, keep_ref, out_ref, low_ref, high_ref, low_t_ref, high_t_ref, weight_ref, taper_ref):
-    members, window = states_ref.shape
-    blocks = window // BLOCK
-    rim = RIM // BLOCK
-    pairs = blocks - 2 * rim
-    fill_taper(taper_ref, members)
-
-    def prepare(block, own):
-        columns = pl.ds(pl.multiple_of(block * BLOCK, BLOCK), BLOCK)
-        prepare_states(states_ref[:, columns], block, own, low_ref, high_ref, low_t_ref, high_t_ref)
-        prepare_weights(weights_ref[:, columns], block, weight_ref)
-
-    pl.loop(0, rim)(lambda b: prepare(b, None))
-    pl.loop(0, pairs)(lambda b: prepare(b + rim, b))
-    pl.loop(0, rim)(lambda b: prepare(b + rim + pairs, None))
-
-    @pl.loop(0, pairs)
-    def _(pair):
-        columns = pl.ds(pl.multiple_of(pair * BLOCK, BLOCK), BLOCK)
-        out_ref[:, columns] = pair_increment(
-            pair, keep_ref, low_ref, high_ref, low_t_ref, high_t_ref, weight_ref, taper_ref
-        )
 
 
 def scratch_of(members, part, pairs):
@@ -189,7 +159,7 @@
         pltpu.VMEM((pairs, BLOCK, members), bf16),
         pltpu.VMEM((blocks, BLOCK, 2 * part), bf16),
         pltpu.VMEM((SPAN, BLOCK, BLOCK), jnp.float32),
-    ]
+    ] + [pltpu.VMEM((BLOCK, SPAN * BLOCK), bf16)] * 4
 
 
 def keep_table_of(neighbours, factor_window, tiles_all):
@@ -201,32 +171,198 @@
     return jnp.sum((shift[:, :, None] == places).astype(jnp.float32), axis=1)
 
 
-def local_increment(states, weights, keep):
-    members, window = states.shape
-    part = weights.shape[0]
-    pairs = window // BLOCK - 2 * (RIM // BLOCK)
-    vmem = pl.BlockSpec(memory_space=pltpu.VMEM)
-    return pl.pallas_call(
-        local_kernel,
-        out_shape=jax.ShapeDtypeStruct((part, pairs * BLOCK), jnp.float32),
-        in_specs=[vmem, vmem, pl.BlockSpec(memory_space=pltpu.SMEM)],
-        out_specs=vmem,
-        scratch_shapes=scratch_of(members, part, pairs),
-        compiler_params=pltpu.CompilerParams(vmem_limit_bytes=60 * 1024 * 1024),
-    )(states, weights, keep)
+def region_kernel(
+    own_ref, weights_ref, factor_ref, keep_ref, out_ref,
+    low_ref, high_ref, low_t_ref, high_t_ref, weight_ref, taper_ref, xh0, xl0, xh1, xl1,
+    held, weight_rim, factor_rim,
+    direct_send, direct_recv, relay_send, relay_recv, rim_send, rim_recv,
+):
+    part, rows = own_ref.shape
+    count = rows // RIM
+    per_chunk = RIM // BLOCK
+    half = part // 2
+    member, region = lax.axis_index("member"), lax.axis_index("region")
+    regions = lax.axis_size("region")
+    beside = member + 1 - 2 * lax.rem(member, 2)
+    across = lax.rem(member + 2, 4)
+    partners = ((beside, region), (across, region))
+    above = (member, lax.rem(region + 1, regions))
+    below = (member, lax.rem(region + regions - 1, regions))
+
+    barrier = pltpu.get_barrier_semaphore()
+    for device in partners + (above, below):
+        pl.semaphore_signal(barrier, inc=1, device_id=device, device_id_type=pl.DeviceIdType.MESH)
+    pl.semaphore_wait(barrier, 4)
+
+    def chunk_at(step):
+        return jnp.where(step == 0, count, step)
+
+    def copy(source, target, send, recv, device):
+        return pltpu.make_async_remote_copy(
+            src_ref=source, dst_ref=target, send_sem=send, recv_sem=recv,
+            device_id=device, device_id_type=pl.DeviceIdType.MESH,
+        )
+
+    def columns_of(chunk):
+        return pl.ds(pl.multiple_of((chunk - 1) * RIM, RIM), RIM)
+
+    def direct(step, side):
+        chunk = chunk_at(step)
+        return copy(
+            own_ref.at[:, columns_of(chunk)], held.at[chunk, 1 + side],
+            direct_send.at[side, step], direct_recv.at[side, step], partners[side],
+        )
+
+    def relay(step, side):
+        chunk = chunk_at(step)
+        strip = pl.ds(side * half, half)
+        return copy(
+            held.at[chunk, 2 - side, strip], held.at[chunk, 3, strip],
+            relay_send.at[side, step], relay_recv.at[side, step], partners[side],
+        )
+
+    def rim(up, item):
+        device = above if up else below
+        edge, place = (count, 0) if up else (1, count + 1)
+        spot = 0 if up else 1
+        columns = slice((edge - 1) * RIM, edge * RIM)
+        if item == 4:
+            source, target = weights_ref.at[:, columns], weight_rim.at[spot]
+        elif item == 5:
+            source, target = factor_ref.at[:, columns], factor_rim.at[spot]
+        elif item == 0:
+            source, target = own_ref.at[:, columns], held.at[place, 0]
+        else:
+            source, target = held.at[edge, item], held.at[place, item]
+        return copy(source, target, rim_send.at[spot, item], rim_recv.at[spot, item], device)
+
+    for step in range(2):
+        for side in range(2):
+            direct(step, side).start()
+    for item in (0, 4, 5):
+        for up in (True, False):
+            rim(up, item).start()
+
+    fill_taper(taper_ref, part * 4)
+
+    @pl.loop(0, count * per_chunk)
+    def _(block):
+        columns = pl.ds(pl.multiple_of(block * BLOCK, BLOCK), BLOCK)
+        prepare_weights(weights_ref[:, columns] * factor_ref[0:1, columns], block + per_chunk, weight_ref)
+
+    def prepare_own(chunk):
+        @pl.loop(0, per_chunk)
+        def _(b):
+            block = (chunk - 1) * per_chunk + b
+            inner = pl.ds(pl.multiple_of(b * BLOCK, BLOCK), BLOCK)
+            mine = own_ref[:, pl.ds(pl.multiple_of(block * BLOCK, BLOCK), BLOCK)]
+            value = jnp.concatenate([mine] + [held[chunk, slot, :, inner] for slot in range(1, 4)], axis=0)
+            prepare_states(value, block + per_chunk, block, low_ref, high_ref, low_t_ref, high_t_ref)
+
+    def prepare_rim(up):
+        place, spot = (0, 0) if up else (count + 1, 1)
+
+        @pl.loop(0, per_chunk)
+        def _(b):
+            inner = pl.ds(pl.multiple_of(b * BLOCK, BLOCK), BLOCK)
+            value = jnp.concatenate([held[place, slot, :, inner] for slot in range(4)], axis=0)
+            block = place * per_chunk + b
+            prepare_states(value, block, None, low_ref, high_ref, low_t_ref, high_t_ref)
+            prepare_weights(weight_rim[spot, :, inner] * factor_rim[spot, 0:1, inner], block, weight_ref)
+
+    @pl.loop(0, count + 3)
+    def _(step):
+        @pl.when(step < count)
+        def _():
+            for side in range(2):
+                direct(step, side).wait_recv()
+            for side in range(2):
+                relay(step, side).start()
+
+        @pl.when(step + 2 < count)
+        def _():
+            for side in range(2):
+                direct(step + 2, side).start()
+
+        for first, up in ((0, True), (1, False)):
+            @pl.when(step == first)
+            def _():
+                for item in (1, 2):
+                    rim(up, item).start()
+
+        @pl.when((step >= 1) & (step <= count))
+        def _():
+            for side in range(2):
+                relay(step - 1, side).wait_recv()
+
+        for first, up in ((1, True), (2, False)):
+            @pl.when(step == first)
+            def _():
+                rim(up, 3).start()
+
+        @pl.when((step >= 1) & (step <= count))
+        def _():
+            prepare_own(chunk_at(step - 1))
+
+        for first, up in ((3, True), (4, False)):
+            @pl.when(step == first)
+            def _():
+                for item in range(6):
+                    rim(up, item).wait_recv()
+                prepare_rim(up)
+
+        @pl.when(step >= 3)
+        def _():
+            @pl.loop(0, per_chunk // 2)
+            def _(b):
+                pair = (step - 3) * per_chunk + 2 * b
+                pair_rows(pair, keep_ref, low_ref, high_ref, low_t_ref, high_t_ref, taper_ref, xh0, xl0)
+                pair_rows(pair + 1, keep_ref, low_ref, high_ref, low_t_ref, high_t_ref, taper_ref, xh1, xl1)
+                columns = pl.ds(pl.multiple_of(pair * BLOCK, BLOCK), BLOCK)
+                out_ref[:, columns] = pair_apply(pair, weight_ref, xh0, xl0)
+                after = pl.ds(pl.multiple_of((pair + 1) * BLOCK, BLOCK), BLOCK)
+                out_ref[:, after] = pair_apply(pair + 1, weight_ref, xh1, xl1)
+
+    @pl.loop(0, count)
+    def _(step):
+        for side in range(2):
+            direct(step, side).wait_send()
+            relay(step, side).wait_send()
+
+    for up in (True, False):
+        for item in range(6):
+            rim(up, item).wait_send()
 
 
 def region_shards(states, weights, obs_count, neighbours):
     region_count = lax.axis_size("region")
     part, local_rows = states.shape
+    members = part * lax.axis_size("member")
+    count = local_rows // RIM
+    pairs = local_rows // BLOCK
     counts = obs_count.astype(jnp.float32)
     factor = counts / (counts + 8.0)
-    scaled = (weights.reshape(part, local_rows // TILE, TILE) * factor[None, :, None]).reshape(part, local_rows)
-    gathered = lax.all_gather(states, "member", axis=0, tiled=True)
-    window = extended_2(gathered, (("region", 1),), RIM)
-    weight_window = extended_2(scaled, (("region", 1),), RIM)
+    factor_rows = jnp.broadcast_to(factor[None, :, None], (8, local_rows // TILE, TILE)).reshape(8, local_rows)
     keep = keep_table_of(neighbours, None, region_count * (local_rows // TILE))
-    return local_increment(window, weight_window, keep)
+    vmem = pl.BlockSpec(memory_space=pltpu.VMEM)
+    dma = pltpu.SemaphoreType.DMA
+    return pl.pallas_call(
+        region_kernel,
+        out_shape=jax.ShapeDtypeStruct((part, local_rows), jnp.float32),
+        in_specs=[vmem, vmem, vmem, pl.BlockSpec(memory_space=pltpu.SMEM)],
+        out_specs=vmem,
+        scratch_shapes=scratch_of(members, part, pairs)
+        + [
+            pltpu.VMEM((count + 2, 4, part, RIM), jnp.float32),
+            pltpu.VMEM((2, part, RIM), jnp.float32),
+            pltpu.VMEM((2, 8, RIM), jnp.float32),
+            dma((2, count)), dma((2, count)), dma((2, count)), dma((2, count)),
+            dma((2, 6)), dma((2, 6)),
+        ],
+        compiler_params=pltpu.CompilerParams(
+            collective_id=0, has_side_effects=True, vmem_limit_bytes=60 * 1024 * 1024
+        ),
+    )(states, weights, factor_rows, keep)
 
 
 def fits(states, weights, obs_count, neighbours):
@@ -234,8 +370,10 @@
     members = part * lax.axis_size("member")
     window = local_rows + 2 * RIM
     return (
-        local_rows % RIM == 0
-        and local_rows >= RIM
+        lax.axis_size("member") == 4
+        and lax.axis_size("region") > 2
+        and local_rows % RIM == 0
+        and local_rows >= 3 * RIM
         and members % 128 == 0
         and part % 64 == 0
         and window * (members * 12 + part * 16) <= 46 * 1024 * 1024

time: 224 us -> 94 us (0.42)
  waiting for transfers between devices: 89.2 us -> 0 us
  between operations: 13.4 us -> 0.02 us
  Pallas kernels: 99.7 us -> 88.3 us
  starting transfers between devices: 8.07 us -> 0 us
  other arithmetic: 7.95 us -> 1.41 us
    all_gather x1 -> x0, waiting for transfers between devices: 68.5 us -> none  [region_shards(): gathered = lax.all_gather(states, 'member', axis=0, tiled=True)]
    ppermute x4 -> x0, waiting for transfers between devices: 19.9 us -> none  [the longest x2 19.9 us: extended_2(): lax.ppermute(lax.slice_in_dim(block, block.shape[dim] - width, None, axis...]
    pallas_call x1, Pallas kernels: 99.7 us -> 88.3 us  [region_shards(): pl.pallas_call(region_kernel, out_shape=jax.ShapeDtypeStruct((part, local...]
    ppermute x4 -> x0, starting transfers between devices: 8.06 us -> none  [the longest x2 7.57 us: extended_2(): lax.ppermute(lax.slice_in_dim(block, 0, width, axis=dim), axis, backward)]
    concatenate x2 -> x0, other arithmetic: 7.13 us -> none  [extended_2(): block = jnp.concatenate([low, block, high], axis=dim)]
    slice x2 -> x0, local copies, waits for them, and re-layouts: 3.87 us -> none  [extended_2(): lax.slice_in_dim(block, block.shape[dim] - width, None, axis=dim)]
    unnamed x4 -> x1, local copies, waits for them, and re-layouts: 0.01 us -> 2.66 us
  transfers between devices with their start and end apart: 5 -> 0, of which waited for: 2 -> 0; matrix products, arithmetic and copies ran while one was open for 3% -> 0% of each run, Pallas kernels for 0% -> 0%
where the time goes in v2:
time: 94 us; the launch traced here: 93.8 us
  Pallas kernels  88.3 us (94%)
  local copies, waits for them, and re-layouts  4.11 us (4%)
  other arithmetic  1.41 us (2%)
    pallas_call x1, Pallas kernels, region_shards(): pl.pallas_call(region_kernel, out_shape=jax.ShapeDtypeStruct((part, local...  88.3 us
    unnamed x1, local copies, waits for them, and re-layouts  2.66 us

profile of v2, /device:TPU:0, one launch (start us, length us, event | category | flops | bytes accessed | tf_op | source)
XLA Modules:
  0.0 93.8 jit_solution(8341584153492496972)
XLA Ops:
  0.0 0.7 add_divide_fusion
  0.7 0.7 add_select_fusion
  1.4 0.7 copy.6.keep_ref
  2.1 0.1 broadcast_bitcast_fusion
  2.2 0.7 broadcast_in_dim.15.factor_ref
  2.9 88.3 %shard_map.46 = f32[64,6144]{1,0:T(8,128)} custom-call(f32[64,6144]{1,0:T(8,128)} %own_ref.1, f32[64,6144]{1,0:T(8,128)} %weights_ref.1, f32[8,6144]{1,0:T(8,128)} %broadcast_in_dim.15.factor_ref, f32[48,20]{1,0:T(8,128)} %copy.6.keep_ref), custom_call_target="tpu_custom_call" | custom-call | tf_op jit(solution)/shard_map/pallas_call | solution.py:349
  91.2 2.7 %copy.8 = f32[64,6144]{1,0:T(8,128)} copy(f32[64,6144]{1,0:T(8,128)} %shard_map.46) | data formatting | bytes 3145728
  (2 shorter events, 0.0 us)

commit v3 on v2

--- a/solution.py
+++ b/solution.py
@@ -127,8 +127,8 @@
     weight_ref[block] = jnp.concatenate([high, value - high], axis=0).T.astype(jnp.bfloat16)
 
 
-def pair_rows(pair, keep_ref, low_ref, high_ref, low_t_ref, high_t_ref, taper_ref, x_high_ref, x_low_ref):
-    for k in range(SPAN):
+def pair_rows(pair, ks, keep_ref, low_ref, high_ref, low_t_ref, high_t_ref, taper_ref, x_high_ref, x_low_ref):
+    for spot, k in enumerate(ks):
         left_high, left_low = high_t_ref[pair], low_t_ref[pair]
         right_high, right_low = high_ref[pair + k], low_ref[pair + k]
         covar = dot(left_high, right_high) + dot(left_low, right_high) + dot(left_high, right_low)
@@ -137,13 +137,14 @@
             for t in range(2):
                 rows, columns = slice(s * TILE, (s + 1) * TILE), slice(t * TILE, (t + 1) * TILE)
                 value = scaled[rows, columns] * keep_ref[2 * pair + s, 2 * k + t + 1 - s]
-                place = slice((2 * k + t) * TILE, (2 * k + t + 1) * TILE)
+                place = slice((2 * spot + t) * TILE, (2 * spot + t + 1) * TILE)
                 x_high_ref[rows, place], x_low_ref[rows, place] = split(value)
 
 
-def pair_apply(pair, weight_ref, x_high_ref, x_low_ref):
-    weight = weight_ref[pl.ds(pair, SPAN)].reshape(SPAN * BLOCK, weight_ref.shape[2])
-    total = dot(x_high_ref[...], weight) + dot(x_low_ref[...], weight)
+def pair_apply(pair, ks, weight_ref, x_high_ref, x_low_ref):
+    depth = len(ks) * BLOCK
+    weight = weight_ref[pl.ds(pair + ks[0], len(ks))].reshape(depth, weight_ref.shape[2])
+    total = dot(x_high_ref[:, :depth], weight) + dot(x_low_ref[:, :depth], weight)
     half = total.shape[1] // 2
     return (total[:, :half] + total[:, half:]).T
 
@@ -195,7 +196,7 @@
     pl.semaphore_wait(barrier, 4)
 
     def chunk_at(step):
-        return jnp.where(step == 0, count, step)
+        return step + 1
 
     def copy(source, target, send, recv, device):
         return pltpu.make_async_remote_copy(
@@ -270,7 +271,21 @@
             prepare_states(value, block, None, low_ref, high_ref, low_t_ref, high_t_ref)
             prepare_weights(weight_rim[spot, :, inner] * factor_rim[spot, 0:1, inner], block, weight_ref)
 
-    @pl.loop(0, count + 3)
+    def work(group, first, last, fresh):
+        buffers = ((xh0, xl0), (xh1, xl1))
+        for start in range(0, per_chunk, 2):
+            todo = []
+            for p in (start, start + 1):
+                ks = [k for k in range(SPAN) if first <= (k + p) // per_chunk <= last]
+                todo.append((group * per_chunk + p, ks, buffers[p % 2]))
+            for pair, ks, held_x in todo:
+                pair_rows(pair, ks, keep_ref, low_ref, high_ref, low_t_ref, high_t_ref, taper_ref, *held_x)
+            for pair, ks, held_x in todo:
+                columns = pl.ds(pl.multiple_of(pair * BLOCK, BLOCK), BLOCK)
+                term = pair_apply(pair, ks, weight_ref, *held_x)
+                out_ref[:, columns] = term if fresh else out_ref[:, columns] + term
+
+    @pl.loop(0, count + 2)
     def _(step):
         @pl.when(step < count)
         def _():
@@ -284,7 +299,7 @@
             for side in range(2):
                 direct(step + 2, side).start()
 
-        for first, up in ((0, True), (1, False)):
+        for first, up in ((0, False), (count - 1, True)):
             @pl.when(step == first)
             def _():
                 for item in (1, 2):
@@ -295,7 +310,7 @@
             for side in range(2):
                 relay(step - 1, side).wait_recv()
 
-        for first, up in ((1, True), (2, False)):
+        for first, up in ((1, False), (count, True)):
             @pl.when(step == first)
             def _():
                 rim(up, 3).start()
@@ -304,24 +319,28 @@
         def _():
             prepare_own(chunk_at(step - 1))
 
-        for first, up in ((3, True), (4, False)):
-            @pl.when(step == first)
-            def _():
-                for item in range(6):
-                    rim(up, item).wait_recv()
-                prepare_rim(up)
-
-        @pl.when(step >= 3)
-        def _():
-            @pl.loop(0, per_chunk // 2)
-            def _(b):
-                pair = (step - 3) * per_chunk + 2 * b
-                pair_rows(pair, keep_ref, low_ref, high_ref, low_t_ref, high_t_ref, taper_ref, xh0, xl0)
-                pair_rows(pair + 1, keep_ref, low_ref, high_ref, low_t_ref, high_t_ref, taper_ref, xh1, xl1)
-                columns = pl.ds(pl.multiple_of(pair * BLOCK, BLOCK), BLOCK)
-                out_ref[:, columns] = pair_apply(pair, weight_ref, xh0, xl0)
-                after = pl.ds(pl.multiple_of((pair + 1) * BLOCK, BLOCK), BLOCK)
-                out_ref[:, after] = pair_apply(pair + 1, weight_ref, xh1, xl1)
+        @pl.when(step == 1)
+        def _():
+            work(0, 1, 1, True)
+
+        @pl.when((step >= 2) & (step <= count))
+        def _():
+            work(step - 1, 0, 1, True)
+
+        @pl.when(step == count + 1)
+        def _():
+            for item in range(6):
+                rim(False, item).wait_recv()
+            prepare_rim(False)
+
+        @pl.when(step >= 2)
+        def _():
+            work(step - 2, 2, 2, False)
+
+    for item in range(6):
+        rim(True, item).wait_recv()
+    prepare_rim(True)
+    work(0, 0, 0, False)
 
     @pl.loop(0, count)
     def _(step):

time: 94 us -> 85.1 us (0.905)
  Pallas kernels: 88.3 us -> 79.4 us
    pallas_call x1, Pallas kernels: 88.3 us -> 79.4 us  [region_shards(): pl.pallas_call(region_kernel, out_shape=jax.ShapeDtypeStruct((part, local...]
where the time goes in v3:
time: 85.1 us; the launch traced here: 84.9 us
  Pallas kernels  79.4 us (93%)
  local copies, waits for them, and re-layouts  4.11 us (5%)
  other arithmetic  1.41 us (2%)
    pallas_call x1, Pallas kernels, region_shards(): pl.pallas_call(region_kernel, out_shape=jax.ShapeDtypeStruct((part, local...  79.4 us
    unnamed x1, local copies, waits for them, and re-layouts  2.66 us

profile of v3, /device:TPU:0, one launch (start us, length us, event | category | flops | bytes accessed | tf_op | source)
XLA Modules:
  0.0 84.9 jit_solution(15311347643558523682)
XLA Ops:
  0.0 0.7 add_divide_fusion
  0.7 0.7 add_select_fusion
  1.4 0.7 copy.6.keep_ref
  2.1 0.1 broadcast_bitcast_fusion
  2.2 0.7 broadcast_in_dim.15.factor_ref
  2.9 79.4 %shard_map.46 = f32[64,6144]{1,0:T(8,128)} custom-call(f32[64,6144]{1,0:T(8,128)} %own_ref.1, f32[64,6144]{1,0:T(8,128)} %weights_ref.1, f32[8,6144]{1,0:T(8,128)} %broadcast_in_dim.15.factor_ref, f32[48,20]{1,0:T(8,128)} %copy.6.keep_ref), custom_call_target="tpu_custom_call" | custom-call | tf_op jit(solution)/shard_map/pallas_call | solution.py:368
  82.3 2.7 %copy.8 = f32[64,6144]{1,0:T(8,128)} copy(f32[64,6144]{1,0:T(8,128)} %shard_map.46) | data formatting | bytes 3145728
  (2 shorter events, 0.0 us)

commit v4 on v3

--- a/solution.py
+++ b/solution.py
@@ -379,7 +379,7 @@
             dma((2, 6)), dma((2, 6)),
         ],
         compiler_params=pltpu.CompilerParams(
-            collective_id=0, has_side_effects=True, vmem_limit_bytes=60 * 1024 * 1024
+            collective_id=0, has_side_effects=True, vmem_limit_bytes=42 * 1024 * 1024
         ),
     )(states, weights, factor_rows, keep)
 

time: 85.1 us -> 83.1 us (0.976)
  Pallas kernels: 79.4 us -> 77.3 us
    pallas_call x1, Pallas kernels: 79.4 us -> 77.3 us  [region_shards(): pl.pallas_call(region_kernel, out_shape=jax.ShapeDtypeStruct((part, local...]
    unnamed x1 -> x5, local copies, waits for them, and re-layouts: 2.66 us -> 3.96 us
where the time goes in v4:
time: 83.1 us; the launch traced here: 82.8 us
  Pallas kernels  77.3 us (93%)
  local copies, waits for them, and re-layouts  4.13 us (5%)
  other arithmetic  1.41 us (2%)
    pallas_call x1, Pallas kernels, region_shards(): pl.pallas_call(region_kernel, out_shape=jax.ShapeDtypeStruct((part, local...  77.3 us
    unnamed x5, local copies, waits for them, and re-layouts  3.96 us

profile of v4, /device:TPU:0, one launch (start us, length us, event | category | flops | bytes accessed | tf_op | source)
XLA Modules:
  0.0 82.8 jit_solution(8576149922906714847)
XLA Ops:
  0.0 0.7 add_divide_fusion
  0.7 0.7 add_select_fusion
  1.4 0.1 copy.6.keep_ref
  1.5 0.1 broadcast_bitcast_fusion
  1.6 0.0 copy-start
  1.6 1.4 %copy-done = f32[64,6144]{1,0:T(8,128)S(1)} copy-done((f32[64,6144]{1,0:T(8,128)S(1)}, f32[64,6144]{1,0:T(8,128)}, u32[]{:S(2)}) %copy-start) | copy-done | bytes 1572888
  3.0 0.0 copy-start.1
  3.0 1.4 %copy-done.1 = f32[64,6144]{1,0:T(8,128)S(1)} copy-done((f32[64,6144]{1,0:T(8,128)S(1)}, f32[64,6144]{1,0:T(8,128)}, u32[]{:S(2)}) %copy-start.1) | copy-done | bytes 1572888
  4.4 77.3 %shard_map.46 = f32[64,6144]{1,0:T(8,128)S(1)} custom-call(f32[64,6144]{1,0:T(8,128)S(1)} %copy-done, f32[64,6144]{1,0:T(8,128)S(1)} %copy-done.1, f32[8,6144]{1,0:T(8,128)S(1)} %broadcast_in_dim.15.factor_ref, f32[48,20]{1,0:T(8,128)S(1)} %copy.6.keep_ref), custom_call_target="tpu_custom_call" | custom-call | tf_op jit(solution)/shard_map/pallas_call | solution.py:368
  81.7 1.1 %copy.8 = f32[64,6144]{1,0:T(8,128)} copy(f32[64,6144]{1,0:T(8,128)S(1)} %shard_map.46) | data formatting | bytes 3145728
  (3 shorter events, 0.0 us)
Async XLA Ops:
  1.6 1.4 %copy-start = (f32[64,6144]{1,0:T(8,128)S(1)}, f32[64,6144]{1,0:T(8,128)}, u32[]{:S(2)}) copy-start(f32[64,6144]{1,0:T(8,128)} %own_ref.1) | copy-start | bytes 4718596
  3.0 1.4 %copy-start.1 = (f32[64,6144]{1,0:T(8,128)S(1)}, f32[64,6144]{1,0:T(8,128)}, u32[]{:S(2)}) copy-start(f32[64,6144]{1,0:T(8,128)} %weights_ref.1) | copy-start | bytes 4718596
